TPU v7x, 32 devices: a whole 2x2x4 slice. The times are simulated.
32 devices in a mesh: groups: 2 (over y), sink: 16 (over z, x, core).
Axes of the slice: x: 2, y: 2, z: 4, core: 2. Of those that a mesh axis runs over, the one named last changes fastest.
Arguments:
- eigvecs: bfloat16 [16, 2, 3, 192, 8192], P('groups', None, None, None, 'sink'), parts along dimension 0
- momentum: int32 [6], P('groups'), parts along dimension 0, may hold values from -5 to 5, as said below
- peram: bfloat16 [32, 2, 768, 768], P(('groups', 'sink')), parts along dimension 0, may hold values from -0.009338379 to 0.009338379
- times: int32 [32, 2], P(('groups', 'sink')), parts along dimension 0, may hold values from 0 to 7, as said below
Outputs:
- blocks: bfloat16 [32, 2, 768, 768], P(('groups', 'sink')), parts along dimension 0
There are 2 independent parts, one for each index of `groups`. A program takes and returns all parts, laid end to end along the dimension named above; each array names one. Nothing has to cross between parts.
Inputs may be any that keep to these rules, and one draw needn't show every extreme that they name: `momentum`: the three components are distinct; one is -5 and one is 5. In each of the two columns every timeslice appears exactly 16 // 8 times.
All inputs are finite; a program needn't handle non-finite values.
Results may differ from a plain program's by a relative error of at most 0.0075.
Values may be sent and summed in bfloat16 or wider, within the bound.
A program may use at most 64 MiB of HBM per device.

v0:
```python
import functools
import math

import jax
import jax.numpy as jnp
from jax import lax
from jax.experimental import pallas as pl
from jax.experimental.pallas import tpu as pltpu
from jax.sharding import PartitionSpec as P

MESH = pl.DeviceIdType.MESH
NT_DIMS = (((1,), (1,)), ((), ()))
GROUP = 2
LAG_CORE = 1
LAG_X = 2
LAG_Z = 3
AHEAD = 4


def angles(momentum, sites, devices, device):
    local = jnp.arange(sites, dtype=jnp.int32)
    second = local // 16
    third = local % 16
    extent = sites // 16
    frac = jnp.mod(momentum[0] * device, devices).astype(jnp.float32) / devices
    frac = frac + jnp.mod(momentum[1] * second, extent).astype(jnp.float32) / extent
    frac = frac + jnp.mod(momentum[2] * third, 16).astype(jnp.float32) / 16.0
    return 2.0 * math.pi * frac


def wrap(value, size):
    if size & (size - 1) == 0:
        return value & (size - 1)
    return lax.rem(lax.rem(value, size) + size, size)


def elemental_kernel(devices, mom_hbm, times_hbm, eig, out, tiles, own1, send1, got1, own2, send2, got2,
                     sendz, gotz, gathered, picked, landed, times_all, mom, times, small_sem, out_sem,
                     load_sem, c_send, c_recv, x_send, x_recv, z_send, z_recv,
                     a_send, a_recv, p_send, p_recv, t_send, t_recv):
    slices, _, colors, width, sites = eig.shape
    planes = devices // 4
    per = slices // planes
    half, quarter = width // 2, width // 4
    me = lax.axis_index("sink")
    c = lax.rem(me, 2)
    x = lax.rem(lax.div(me, 2), 2)
    z = lax.div(me, 4)
    q = 2 * c + x

    def at(zz, xx, cc):
        return {"sink": (zz * 2 + xx) * 2 + cc}

    core_mate = at(z, x, 1 - c)
    x_mate = at(z, 1 - x, c)
    mates = [(1 - x, c), (x, 1 - c), (1 - x, 1 - c)]
    others = [lax.rem(z + k, planes) for k in range(1, planes)]

    upper = lax.div(z, 2)
    order = [3 * (1 - upper), 2 - upper, z + 1 - 2 * lax.rem(z, 2), z]
    steps = [(order[s], j) for j in range(per) for s in range(planes)]
    count = len(steps)

    mom_load = pltpu.make_async_copy(mom_hbm, mom, small_sem.at[0])
    mom_load.start()
    times_load = pltpu.make_async_copy(times_hbm, times, small_sem.at[1])
    times_load.start()
    loads = []
    for i, (zt, j) in enumerate(steps):
        load = pltpu.make_async_copy(eig.at[zt * per + j], tiles.at[i], load_sem.at[i])
        loads.append(load)
        if i < AHEAD:
            load.start()

    barrier = pltpu.get_barrier_semaphore()
    for xx, cc in mates:
        pl.semaphore_signal(barrier, inc=1, device_id=at(z, xx, cc), device_id_type=MESH)
    for zz in others:
        pl.semaphore_signal(barrier, inc=1, device_id=at(zz, x, c), device_id_type=MESH)

    mom_load.wait()
    extent = sites // 16
    local = lax.broadcasted_iota(jnp.int32, (8, sites), 1)
    second = local >> 4
    third = local & 15
    first = wrap(mom[0] * me, devices).astype(jnp.float32) / devices
    frac = first + wrap(mom[1] * second, extent).astype(jnp.float32) / extent
    frac = frac + wrap(mom[2] * third, 16).astype(jnp.float32) / 16.0
    theta = (2.0 * math.pi) * frac
    cosine = jnp.cos(theta)[0:1]
    sine = jnp.sin(theta)[0:1]

    def remote(src, dst, ssem, rsem, dev):
        return pltpu.make_async_remote_copy(src_ref=src, dst_ref=dst, send_sem=ssem, recv_sem=rsem,
                                            device_id=dev, device_id_type=MESH)

    sends = []
    core_copies, x_copies = [], []

    def partial_sum(i):
        r_re, r_im, v_all = [], [], []
        for col in range(colors):
            v_re = tiles[i, 0, col]
            v_im = tiles[i, 1, col]
            f_re = v_re.astype(jnp.float32)
            f_im = v_im.astype(jnp.float32)
            r_re.append((cosine * f_re + sine * f_im).astype(jnp.bfloat16))
            r_im.append((cosine * f_im - sine * f_re).astype(jnp.bfloat16))
            v_all.append(jnp.concatenate([v_re, v_im], axis=0))
        both = jnp.concatenate(v_all, axis=1)
        r_re = jnp.concatenate(r_re, axis=1)
        r_im = jnp.concatenate(r_im, axis=1)
        by_re = lax.dot_general(both, r_re, NT_DIMS, preferred_element_type=jnp.float32)
        by_im = lax.dot_general(both, r_im, NT_DIMS, preferred_element_type=jnp.float32)
        real = by_re[:width] + by_im[width:]
        imag = by_im[:width] - by_re[width:]
        total = jnp.concatenate([real, imag], axis=1)
        own1[i] = total
        send1[i] = total.astype(jnp.bfloat16)

    def start_core(i):
        rows = pl.ds(pl.multiple_of((1 - c) * half, half), half)
        copy = remote(send1.at[i, rows], got1.at[i], c_send.at[i], c_recv.at[i], core_mate)
        copy.start()
        core_copies.append(copy)
        sends.append(copy)

    def core_stage(i):
        core_copies[i].wait_recv()
        total = own1[i, pl.ds(pl.multiple_of(c * half, half), half)] + got1[i].astype(jnp.float32)
        own2[i] = total
        send2[i] = total.astype(jnp.bfloat16)
        rows = pl.ds(pl.multiple_of((1 - x) * quarter, quarter), quarter)
        copy = remote(send2.at[i, rows], got2.at[i], x_send.at[i], x_recv.at[i], x_mate)
        copy.start()
        x_copies.append(copy)
        sends.append(copy)

    mine = []

    def x_stage(i):
        zt, j = steps[i]
        x_copies[i].wait_recv()
        total = own2[i, pl.ds(pl.multiple_of(x * quarter, quarter), quarter)] + got2[i].astype(jnp.float32)
        if i % planes < planes - 1:
            sendz[i] = total.astype(jnp.bfloat16)
            copy = remote(sendz.at[i], gotz.at[z, j], z_send.at[i], z_recv.at[z, j], at(zt, x, c))
            copy.start()
            sends.append(copy)
        else:
            mine.append(total)

    def finish(j):
        total = mine[j]
        for zz in others:
            remote(sendz.at[0], gotz.at[zz, j], z_send.at[0], z_recv.at[zz, j], at(zz, x, c)).wait_recv()
            total = total + gotz[zz, j].astype(jnp.float32)
        gathered[z * per + j] = total.astype(jnp.bfloat16)
        block = gathered.at[z * per + j]
        for k in reversed(range(len(others))):
            zz = others[k]
            copy = remote(block, block, a_send.at[k, j], a_recv.at[z, j], at(zz, x, c))
            copy.start()
            sends.append(copy)

    groups = count // GROUP

    def members(g):
        return range(g * GROUP, (g + 1) * GROUP) if 0 <= g < groups else ()

    for g in range(groups + LAG_Z):
        for i in members(g):
            loads[i].wait()
            if i + AHEAD < count:
                loads[i + AHEAD].start()
        for i in members(g):
            partial_sum(i)
        if g == 0:
            pl.semaphore_wait(barrier, len(mates) + len(others))
            times_load.wait()
            for m, (xx, cc) in enumerate(mates):
                copy = remote(times, times_all.at[q], t_send.at[m], t_recv.at[q], at(z, xx, cc))
                copy.start()
                sends.append(copy)
        for i in members(g):
            start_core(i)
        for i in members(g - LAG_CORE):
            core_stage(i)
        for i in members(g - LAG_X):
            x_stage(i)
        for i in members(g - LAG_Z):
            if i % planes == planes - 1:
                finish(i // planes)

    for j in range(per):
        for zz in others:
            there = gathered.at[zz * per + j]
            remote(there, there, a_send.at[0, j], a_recv.at[zz, j], at(zz, x, c)).wait_recv()

    for m, (xx, cc) in enumerate(mates):
        other = 2 * cc + xx
        remote(times, times_all.at[other], t_send.at[m], t_recv.at[other], at(z, xx, cc)).wait_recv()
        for w in range(2):
            picked[m, w] = gathered[times_all[other, 0, w]]
        copy = remote(picked.at[m], landed.at[q], p_send.at[m], p_recv.at[q], at(z, xx, cc))
        copy.start()
        sends.append(copy)
    for w in range(2):
        landed[q, w] = gathered[times[0, w]]
    for m, (xx, cc) in enumerate(mates):
        other = 2 * cc + xx
        remote(picked.at[m], landed.at[other], p_send.at[m], p_recv.at[other], at(z, xx, cc)).wait_recv()
    stores = []
    for r in range(4):
        store = pltpu.make_async_copy(landed.at[r], out.at[:, pl.ds(r * quarter, quarter)], out_sem.at[r])
        store.start()
        stores.append(store)
    for store in stores:
        store.wait()
    for copy in sends:
        copy.wait_send()


def pair_elementals(eigvecs, momentum, times, devices):
    slices, _, colors, width, sites = eigvecs.shape
    planes = devices // 4
    per = slices // planes
    half, quarter, both = width // 2, width // 4, 2 * width
    bf, f32 = jnp.bfloat16, jnp.float32
    dma = pltpu.SemaphoreType.DMA
    return pl.pallas_call(
        functools.partial(elemental_kernel, devices),
        out_shape=jax.ShapeDtypeStruct((2, width, both), bf),
        in_specs=[
            pl.BlockSpec(memory_space=pltpu.HBM),
            pl.BlockSpec(memory_space=pltpu.HBM),
            pl.BlockSpec(memory_space=pltpu.HBM),
        ],
        out_specs=pl.BlockSpec(memory_space=pltpu.HBM),
        scratch_shapes=[
            pltpu.VMEM((slices, 2, colors, width, sites), bf),
            pltpu.VMEM((slices, width, both), f32),
            pltpu.VMEM((slices, width, both), bf),
            pltpu.VMEM((slices, half, both), bf),
            pltpu.VMEM((slices, half, both), f32),
            pltpu.VMEM((slices, half, both), bf),
            pltpu.VMEM((slices, quarter, both), bf),
            pltpu.VMEM((slices, quarter, both), bf),
            pltpu.VMEM((planes, per, quarter, both), bf),
            pltpu.VMEM((slices, quarter, both), bf),
            pltpu.VMEM((3, 2, quarter, both), bf),
            pltpu.VMEM((4, 2, quarter, both), bf),
            pltpu.SMEM((4, 1, 2), jnp.int32),
            pltpu.SMEM(momentum.shape, jnp.int32),
            pltpu.SMEM(times.shape, jnp.int32),
            dma((2,)),
            dma((4,)),
            dma((slices,)),
            dma((slices,)), dma((slices,)), dma((slices,)), dma((slices,)),
            dma((slices,)), dma((planes, per)),
            dma((planes, per)), dma((planes, per)),
            dma((3,)), dma((4,)),
            dma((3,)), dma((4,)),
        ],
        compiler_params=pltpu.CompilerParams(
            collective_id=0, has_side_effects=True, vmem_limit_bytes=67043328
        ),
    )(momentum, times, eigvecs)


def blocks_kernel(elementals, peram, out, left, right):
    width = elementals.shape[1]
    step = pl.program_id(0)

    @pl.when(step == 0)
    def _():
        a_re = elementals[0][:, :width]
        a_im = elementals[0][:, width:]
        left[:width] = jnp.concatenate([a_re, -a_im], axis=1)
        left[width:] = jnp.concatenate([a_im, a_re], axis=1)
        e_re = elementals[1][:, :width]
        e_im = elementals[1][:, width:]
        right[0] = e_re
        right[1] = e_im

    stacked = peram[0].reshape(2 * width, peram.shape[-1])
    x = jnp.dot(left[...], stacked, preferred_element_type=jnp.float32)
    sign = jnp.where(step < 2, 1.0, -1.0).astype(jnp.float32)
    x = (x * sign).astype(jnp.bfloat16)
    reals, imags = [], []
    for b in range(4):
        s = (b + 2) % 4
        piece = x[:, s * width:(s + 1) * width]
        by_re = lax.dot_general(piece, right[0], NT_DIMS, preferred_element_type=jnp.float32)
        by_im = lax.dot_general(piece, right[1], NT_DIMS, preferred_element_type=jnp.float32)
        reals.append(by_re[:width] + by_im[width:])
        imags.append(by_re[width:] - by_im[:width])
    out[0, 0] = jnp.concatenate(reals, axis=1).astype(jnp.bfloat16)
    out[0, 1] = jnp.concatenate(imags, axis=1).astype(jnp.bfloat16)


def meson_blocks(elementals, peram):
    width = elementals.shape[1]
    return pl.pallas_call(
        blocks_kernel,
        grid=(4,),
        out_shape=jax.ShapeDtypeStruct(peram.shape, peram.dtype),
        in_specs=[
            pl.BlockSpec(elementals.shape, lambda i: (0, 0, 0)),
            pl.BlockSpec((1, 2, width, 4 * width), lambda i: (0, 0, (i + 2) % 4, 0)),
        ],
        out_specs=pl.BlockSpec((1, 2, width, 4 * width), lambda i: (0, 0, i, 0)),
        scratch_shapes=[
            pltpu.VMEM((2 * width, 2 * width), jnp.bfloat16),
            pltpu.VMEM((2, width, width), jnp.bfloat16),
        ],
        compiler_params=pltpu.CompilerParams(vmem_limit_bytes=67043328),
    )(elementals, peram)


def summed_elementals(eigvecs, momentum, times, devices):
    device = lax.axis_index("sink")
    theta = angles(momentum, eigvecs.shape[-1], devices, device)
    cosine = jnp.cos(theta)
    sine = jnp.sin(theta)
    vec_re = eigvecs[:, 0]
    vec_im = eigvecs[:, 1]
    f_re = vec_re.astype(jnp.float32)
    f_im = vec_im.astype(jnp.float32)
    rot_re = (cosine * f_re + sine * f_im).astype(jnp.bfloat16)
    rot_im = (cosine * f_im - sine * f_re).astype(jnp.bfloat16)
    form = "tckx,tclx->tkl"
    dot = functools.partial(jnp.einsum, form, preferred_element_type=jnp.float32)
    real = dot(vec_re, rot_re) + dot(vec_im, rot_im)
    imag = dot(vec_re, rot_im) - dot(vec_im, rot_re)
    totals = lax.psum(jnp.concatenate([real, imag], axis=-1), "sink")
    return jnp.take(totals.astype(jnp.bfloat16), times[0], axis=0)


def shards(eigvecs, momentum, peram, times):
    devices = lax.axis_size("sink")
    if devices == 16 and eigvecs.shape[0] % 8 == 0:
        elementals = pair_elementals(eigvecs, momentum, times, devices)
    else:
        elementals = summed_elementals(eigvecs, momentum, times, devices)
    return meson_blocks(elementals, peram)


def solution(mesh):
    in_specs = (
        P("groups", None, None, None, "sink"),
        P("groups"),
        P(("groups", "sink"), None, None, None),
        P(("groups", "sink"), None),
    )
    out_specs = P(("groups", "sink"), None, None, None)
    return jax.shard_map(shards, mesh=mesh, in_specs=in_specs, out_specs=out_specs, check_vma=False)
```

profile of v0, /device:TPU:1, one launch (start us, length us, event | category | flops | bytes accessed | tf_op | source)
XLA Modules:
  0.0 38.1 jit_solution(2445739946190257706)
XLA Ops:
  0.0 31.4 %shard_map.46.elementals = bf16[2,192,384]{2,1,0:T(8,128)(2,1)} custom-call(s32[3]{0:T(128)} %mom_hbm.1, s32[1,2]{1,0:T(1,128)} %times_hbm.1, bf16[8,2,3,192,512]{4,3,2,1,0:T(8,128)(2,1)} %eig.1), custom_call_target="tpu_custom_call" | custom-call | tf_op jit(solution)/shard_map/pallas_call | solution.py:231
  31.4 6.7 %shard_map.47 = bf16[1,2,768,768]{3,2,1,0:T(8,128)(2,1)} custom-call(bf16[2,192,384]{2,1,0:T(8,128)(2,1)} %shard_map.46.elementals, bf16[1,2,768,768]{3,2,1,0:T(8,128)(2,1)} %peram.1), custom_call_target="tpu_custom_call" | custom-call | tf_op jit(solution)/shard_map/pallas_call | solution.py:304
where the time goes:
time: 38.3 us; the launch traced here: 38.1 us
  Pallas kernels  38.1 us (99%)
    pallas_call x1, Pallas kernels, pair_elementals(): pl.pallas_call(functools.partial(elemental_kernel, devices), out_shape=ja...  31.4 us
    pallas_call x1, Pallas kernels, meson_blocks(): pl.pallas_call(blocks_kernel, grid=(4,), out_shape=jax.ShapeDtypeStruct(p...  6.72 us

commit v1 on v0

--- a/solution.py
+++ b/solution.py
@@ -10,10 +10,8 @@
 
 MESH = pl.DeviceIdType.MESH
 NT_DIMS = (((1,), (1,)), ((), ()))
-GROUP = 2
 LAG_CORE = 1
-LAG_X = 2
-LAG_Z = 3
+LAG_X = 4
 AHEAD = 4
 
 
@@ -34,8 +32,8 @@
     return lax.rem(lax.rem(value, size) + size, size)
 
 
-def elemental_kernel(devices, mom_hbm, times_hbm, eig, out, tiles, own1, send1, got1, own2, send2, got2,
-                     sendz, gotz, gathered, picked, landed, times_all, mom, times, small_sem, out_sem,
+def elemental_kernel(devices, mom_hbm, times_hbm, eig, landed, tiles, own1, send1, got1, own2, send2, got2,
+                     sendz, gotz, gathered, picked, times_all, mom, times, small_sem,
                      load_sem, c_send, c_recv, x_send, x_recv, z_send, z_recv,
                      a_send, a_recv, p_send, p_recv, t_send, t_recv):
     slices, _, colors, width, sites = eig.shape
@@ -43,9 +41,9 @@
     per = slices // planes
     half, quarter = width // 2, width // 4
     me = lax.axis_index("sink")
-    c = lax.rem(me, 2)
     x = lax.rem(lax.div(me, 2), 2)
     z = lax.div(me, 4)
+    c = me & 1
     q = 2 * c + x
 
     def at(zz, xx, cc):
@@ -98,22 +96,23 @@
     core_copies, x_copies = [], []
 
     def partial_sum(i):
-        r_re, r_im, v_all = [], [], []
+        rot_re, rot_im, neg_re, vec_re, vec_im = [], [], [], [], []
         for col in range(colors):
             v_re = tiles[i, 0, col]
             v_im = tiles[i, 1, col]
             f_re = v_re.astype(jnp.float32)
             f_im = v_im.astype(jnp.float32)
-            r_re.append((cosine * f_re + sine * f_im).astype(jnp.bfloat16))
-            r_im.append((cosine * f_im - sine * f_re).astype(jnp.bfloat16))
-            v_all.append(jnp.concatenate([v_re, v_im], axis=0))
-        both = jnp.concatenate(v_all, axis=1)
-        r_re = jnp.concatenate(r_re, axis=1)
-        r_im = jnp.concatenate(r_im, axis=1)
-        by_re = lax.dot_general(both, r_re, NT_DIMS, preferred_element_type=jnp.float32)
-        by_im = lax.dot_general(both, r_im, NT_DIMS, preferred_element_type=jnp.float32)
-        real = by_re[:width] + by_im[width:]
-        imag = by_im[:width] - by_re[width:]
+            r_re = (cosine * f_re + sine * f_im).astype(jnp.bfloat16)
+            rot_re.append(r_re)
+            neg_re.append(-r_re)
+            rot_im.append((cosine * f_im - sine * f_re).astype(jnp.bfloat16))
+            vec_re.append(v_re)
+            vec_im.append(v_im)
+        both = jnp.concatenate(vec_re + vec_im, axis=1)
+        for_re = jnp.concatenate(rot_re + rot_im, axis=1)
+        for_im = jnp.concatenate(rot_im + neg_re, axis=1)
+        real = lax.dot_general(both, for_re, NT_DIMS, preferred_element_type=jnp.float32)
+        imag = lax.dot_general(both, for_im, NT_DIMS, preferred_element_type=jnp.float32)
         total = jnp.concatenate([real, imag], axis=1)
         own1[i] = total
         send1[i] = total.astype(jnp.bfloat16)
@@ -163,34 +162,36 @@
             copy.start()
             sends.append(copy)
 
-    groups = count // GROUP
-
-    def members(g):
-        return range(g * GROUP, (g + 1) * GROUP) if 0 <= g < groups else ()
-
-    for g in range(groups + LAG_Z):
-        for i in members(g):
-            loads[i].wait()
-            if i + AHEAD < count:
-                loads[i + AHEAD].start()
-        for i in members(g):
-            partial_sum(i)
-        if g == 0:
+    last = count - 1
+
+    def after(i):
+        start_core(i)
+        if i >= LAG_CORE:
+            core_stage(i - LAG_CORE)
+        if i >= LAG_X:
+            x_stage(i - LAG_X)
+
+    for i in range(count):
+        loads[i].wait()
+        if i + AHEAD < count:
+            loads[i + AHEAD].start()
+        partial_sum(i)
+        if i == 0:
             pl.semaphore_wait(barrier, len(mates) + len(others))
             times_load.wait()
             for m, (xx, cc) in enumerate(mates):
                 copy = remote(times, times_all.at[q], t_send.at[m], t_recv.at[q], at(z, xx, cc))
                 copy.start()
                 sends.append(copy)
-        for i in members(g):
-            start_core(i)
-        for i in members(g - LAG_CORE):
-            core_stage(i)
-        for i in members(g - LAG_X):
-            x_stage(i)
-        for i in members(g - LAG_Z):
-            if i % planes == planes - 1:
-                finish(i // planes)
+        after(i)
+    for i in range(count - LAG_CORE, count):
+        core_stage(i)
+    for i in range(count - LAG_X, count):
+        x_stage(i)
+        if i == count - LAG_X + 1:
+            for j in range(per - 1):
+                finish(j)
+    finish(per - 1)
 
     for j in range(per):
         for zz in others:
@@ -210,13 +211,6 @@
     for m, (xx, cc) in enumerate(mates):
         other = 2 * cc + xx
         remote(picked.at[m], landed.at[other], p_send.at[m], p_recv.at[other], at(z, xx, cc)).wait_recv()
-    stores = []
-    for r in range(4):
-        store = pltpu.make_async_copy(landed.at[r], out.at[:, pl.ds(r * quarter, quarter)], out_sem.at[r])
-        store.start()
-        stores.append(store)
-    for store in stores:
-        store.wait()
     for copy in sends:
         copy.wait_send()
 
@@ -230,13 +224,13 @@
     dma = pltpu.SemaphoreType.DMA
     return pl.pallas_call(
         functools.partial(elemental_kernel, devices),
-        out_shape=jax.ShapeDtypeStruct((2, width, both), bf),
+        out_shape=jax.ShapeDtypeStruct((4, 2, quarter, both), bf),
         in_specs=[
             pl.BlockSpec(memory_space=pltpu.HBM),
             pl.BlockSpec(memory_space=pltpu.HBM),
             pl.BlockSpec(memory_space=pltpu.HBM),
         ],
-        out_specs=pl.BlockSpec(memory_space=pltpu.HBM),
+        out_specs=pl.BlockSpec(memory_space=pltpu.VMEM),
         scratch_shapes=[
             pltpu.VMEM((slices, 2, colors, width, sites), bf),
             pltpu.VMEM((slices, width, both), f32),
@@ -249,12 +243,10 @@
             pltpu.VMEM((planes, per, quarter, both), bf),
             pltpu.VMEM((slices, quarter, both), bf),
             pltpu.VMEM((3, 2, quarter, both), bf),
-            pltpu.VMEM((4, 2, quarter, both), bf),
             pltpu.SMEM((4, 1, 2), jnp.int32),
             pltpu.SMEM(momentum.shape, jnp.int32),
             pltpu.SMEM(times.shape, jnp.int32),
             dma((2,)),
-            dma((4,)),
             dma((slices,)),
             dma((slices,)), dma((slices,)), dma((slices,)), dma((slices,)),
             dma((slices,)), dma((planes, per)),
@@ -263,58 +255,57 @@
             dma((3,)), dma((4,)),
         ],
         compiler_params=pltpu.CompilerParams(
-            collective_id=0, has_side_effects=True, vmem_limit_bytes=67043328
+            collective_id=0, has_side_effects=True, vmem_limit_bytes=25165824
         ),
-    )(momentum, times, eigvecs)
-
-
-def blocks_kernel(elementals, peram, out, left, right):
-    width = elementals.shape[1]
-    step = pl.program_id(0)
-
-    @pl.when(step == 0)
-    def _():
-        a_re = elementals[0][:, :width]
-        a_im = elementals[0][:, width:]
-        left[:width] = jnp.concatenate([a_re, -a_im], axis=1)
-        left[width:] = jnp.concatenate([a_im, a_re], axis=1)
-        e_re = elementals[1][:, :width]
-        e_im = elementals[1][:, width:]
-        right[0] = e_re
-        right[1] = e_im
-
-    stacked = peram[0].reshape(2 * width, peram.shape[-1])
-    x = jnp.dot(left[...], stacked, preferred_element_type=jnp.float32)
-    sign = jnp.where(step < 2, 1.0, -1.0).astype(jnp.float32)
-    x = (x * sign).astype(jnp.bfloat16)
-    reals, imags = [], []
-    for b in range(4):
-        s = (b + 2) % 4
-        piece = x[:, s * width:(s + 1) * width]
-        by_re = lax.dot_general(piece, right[0], NT_DIMS, preferred_element_type=jnp.float32)
-        by_im = lax.dot_general(piece, right[1], NT_DIMS, preferred_element_type=jnp.float32)
-        reals.append(by_re[:width] + by_im[width:])
-        imags.append(by_re[width:] - by_im[:width])
-    out[0, 0] = jnp.concatenate(reals, axis=1).astype(jnp.bfloat16)
-    out[0, 1] = jnp.concatenate(imags, axis=1).astype(jnp.bfloat16)
+    )(*(pltpu.with_memory_space_constraint(v, pltpu.HBM) for v in (momentum, times, eigvecs)))
+
+
+def blocks_kernel(elementals, peram, out, staged, done):
+    width = elementals.shape[3] // 2
+    sink_el = jnp.concatenate([elementals[r, 0] for r in range(4)], axis=0)
+    src_el = jnp.concatenate([elementals[r, 1] for r in range(4)], axis=0)
+    a_re = sink_el[:, :width]
+    a_im = sink_el[:, width:]
+    upper = jnp.concatenate([a_re, -a_im], axis=1)
+    lower = jnp.concatenate([a_im, a_re], axis=1)
+    left = jnp.concatenate([upper, lower], axis=0)
+    e_re = src_el[:, :width]
+    e_im = src_el[:, width:]
+    stores = []
+    for a in range(4):
+        rows = pl.ds((a + 2) % 4 * width, width)
+        stacked = jnp.concatenate([peram[0, 0, rows], peram[0, 1, rows]], axis=0)
+        x = jnp.dot(left, stacked, preferred_element_type=jnp.float32)
+        x = (x if a < 2 else -x).astype(jnp.bfloat16)
+        reals, imags = [], []
+        for b in range(4):
+            s = (b + 2) % 4
+            piece = x[:, s * width:(s + 1) * width]
+            by_re = lax.dot_general(piece, e_re, NT_DIMS, preferred_element_type=jnp.float32)
+            by_im = lax.dot_general(piece, e_im, NT_DIMS, preferred_element_type=jnp.float32)
+            reals.append(by_re[:width] + by_im[width:])
+            imags.append(by_re[width:] - by_im[:width])
+        here = pl.ds(a * width, width)
+        staged[0, here] = jnp.concatenate(reals, axis=1).astype(jnp.bfloat16)
+        staged[1, here] = jnp.concatenate(imags, axis=1).astype(jnp.bfloat16)
+        store = pltpu.make_async_copy(staged.at[:, here], out.at[0, :, here], done.at[a])
+        store.start()
+        stores.append(store)
+    for store in stores:
+        store.wait()
 
 
 def meson_blocks(elementals, peram):
-    width = elementals.shape[1]
     return pl.pallas_call(
         blocks_kernel,
-        grid=(4,),
         out_shape=jax.ShapeDtypeStruct(peram.shape, peram.dtype),
-        in_specs=[
-            pl.BlockSpec(elementals.shape, lambda i: (0, 0, 0)),
-            pl.BlockSpec((1, 2, width, 4 * width), lambda i: (0, 0, (i + 2) % 4, 0)),
+        in_specs=[pl.BlockSpec(memory_space=pltpu.VMEM), pl.BlockSpec(memory_space=pltpu.VMEM)],
+        out_specs=pl.BlockSpec(memory_space=pltpu.HBM),
+        scratch_shapes=[
+            pltpu.VMEM(peram.shape[1:], peram.dtype),
+            pltpu.SemaphoreType.DMA((4,)),
         ],
-        out_specs=pl.BlockSpec((1, 2, width, 4 * width), lambda i: (0, 0, i, 0)),
-        scratch_shapes=[
-            pltpu.VMEM((2 * width, 2 * width), jnp.bfloat16),
-            pltpu.VMEM((2, width, width), jnp.bfloat16),
-        ],
-        compiler_params=pltpu.CompilerParams(vmem_limit_bytes=67043328),
+        compiler_params=pltpu.CompilerParams(vmem_limit_bytes=25165824),
     )(elementals, peram)
 
 
@@ -334,7 +325,9 @@
     real = dot(vec_re, rot_re) + dot(vec_im, rot_im)
     imag = dot(vec_re, rot_im) - dot(vec_im, rot_re)
     totals = lax.psum(jnp.concatenate([real, imag], axis=-1), "sink")
-    return jnp.take(totals.astype(jnp.bfloat16), times[0], axis=0)
+    picked = jnp.take(totals.astype(jnp.bfloat16), times[0], axis=0)
+    quarter = picked.shape[1] // 4
+    return picked.reshape(2, 4, quarter, picked.shape[2]).transpose(1, 0, 2, 3)
 
 
 def shards(eigvecs, momentum, peram, times):

time: 38.3 us -> 35.1 us (0.916)
  Pallas kernels: 38.1 us -> 35 us
    pallas_call x1, Pallas kernels: 6.72 us -> 4.57 us  [meson_blocks(): pl.pallas_call(blocks_kernel, out_shape=jax.ShapeDtypeStruct(peram.shape,...]
    pallas_call x1, Pallas kernels: 31.4 us -> 30.4 us  [pair_elementals(): pl.pallas_call(functools.partial(elemental_kernel, devices), out_shape=ja...]
where the time goes in v1:
time: 35.1 us; the launch traced here: 35 us
  Pallas kernels  35 us (100%)
    pallas_call x1, Pallas kernels, pair_elementals(): pl.pallas_call(functools.partial(elemental_kernel, devices), out_shape=ja...  30.4 us
    pallas_call x1, Pallas kernels, meson_blocks(): pl.pallas_call(blocks_kernel, out_shape=jax.ShapeDtypeStruct(peram.shape,...  4.57 us

profile of v1, /device:TPU:1, one launch (start us, length us, event | category | flops | bytes accessed | tf_op | source)
XLA Modules:
  0.0 35.0 jit_solution(17309125583119954862)
XLA Ops:
  0.0 0.0 copy-start
  0.0 30.4 %shard_map.46.elementals = bf16[4,2,48,384]{3,2,1,0:T(8,128)(2,1)S(1)} custom-call(s32[3]{0:T(128)} %mom_hbm.1, s32[1,2]{1,0:T(1,128)} %times_hbm.1, bf16[8,2,3,192,512]{4,3,2,1,0:T(8,128)(2,1)} %eig.1), custom_call_target="tpu_custom_call" | custom-call | tf_op jit(solution)/shard_map/pallas_call | solution.py:225
  30.4 0.0 copy-done
  30.4 4.6 %shard_map.47 = bf16[1,2,768,768]{3,2,1,0:T(8,128)(2,1)} custom-call(bf16[4,2,48,384]{3,2,1,0:T(8,128)(2,1)S(1)} %shard_map.46.elementals, bf16[1,2,768,768]{3,2,1,0:T(8,128)(2,1)S(1)} %copy-done), custom_call_target="tpu_custom_call" | custom-call | tf_op jit(solution)/shard_map/pallas_call | solution.py:299
Async XLA Ops:
  0.0 30.4 %copy-start = (bf16[1,2,768,768]{3,2,1,0:T(8,128)(2,1)S(1)}, bf16[1,2,768,768]{3,2,1,0:T(8,128)(2,1)}, u32[]{:S(2)}) copy-start(bf16[1,2,768,768]{3,2,1,0:T(8,128)(2,1)} %peram.1) | copy-start | bytes 7077892

commit v2 on v1

--- a/solution.py
+++ b/solution.py
@@ -33,12 +33,11 @@
 
 
 def elemental_kernel(devices, mom_hbm, times_hbm, eig, landed, tiles, own1, send1, got1, own2, send2, got2,
-                     sendz, gotz, gathered, picked, times_all, mom, times, small_sem,
-                     load_sem, c_send, c_recv, x_send, x_recv, z_send, z_recv,
+                     sendz, gotz, own3, sendf, gotf, gathered, picked, times_all, mom, times, small_sem,
+                     load_sem, c_send, c_recv, x_send, x_recv, z_send, z_recv, f_send, f_recv,
                      a_send, a_recv, p_send, p_recv, t_send, t_recv):
     slices, _, colors, width, sites = eig.shape
-    planes = devices // 4
-    per = slices // planes
+    own = slices // 2
     half, quarter = width // 2, width // 4
     me = lax.axis_index("sink")
     x = lax.rem(lax.div(me, 2), 2)
@@ -52,11 +51,14 @@
     core_mate = at(z, x, 1 - c)
     x_mate = at(z, 1 - x, c)
     mates = [(1 - x, c), (x, 1 - c), (1 - x, 1 - c)]
-    others = [lax.rem(z + k, planes) for k in range(1, planes)]
-
-    upper = lax.div(z, 2)
-    order = [3 * (1 - upper), 2 - upper, z + 1 - 2 * lax.rem(z, 2), z]
-    steps = [(order[s], j) for j in range(per) for s in range(planes)]
+
+    parity = lax.rem(z, 2)
+    near = at(z + 1 - 2 * parity, x, c)
+    far = at(lax.rem(z + 2, 4), x, c)
+    mine = parity * own
+    theirs = (1 - parity) * own
+
+    steps = [theirs + k for k in range(own)] + [mine + k for k in range(own)]
     count = len(steps)
 
     mom_load = pltpu.make_async_copy(mom_hbm, mom, small_sem.at[0])
@@ -64,8 +66,8 @@
     times_load = pltpu.make_async_copy(times_hbm, times, small_sem.at[1])
     times_load.start()
     loads = []
-    for i, (zt, j) in enumerate(steps):
-        load = pltpu.make_async_copy(eig.at[zt * per + j], tiles.at[i], load_sem.at[i])
+    for i, slot in enumerate(steps):
+        load = pltpu.make_async_copy(eig.at[slot], tiles.at[i], load_sem.at[i])
         loads.append(load)
         if i < AHEAD:
             load.start()
@@ -73,8 +75,8 @@
     barrier = pltpu.get_barrier_semaphore()
     for xx, cc in mates:
         pl.semaphore_signal(barrier, inc=1, device_id=at(z, xx, cc), device_id_type=MESH)
-    for zz in others:
-        pl.semaphore_signal(barrier, inc=1, device_id=at(zz, x, c), device_id_type=MESH)
+    for other in (near, far):
+        pl.semaphore_signal(barrier, inc=1, device_id=other, device_id_type=MESH)
 
     mom_load.wait()
     extent = sites // 16
@@ -135,34 +137,35 @@
         x_copies.append(copy)
         sends.append(copy)
 
-    mine = []
+    def from_near(k):
+        return remote(sendz.at[k], gotz.at[k], z_send.at[k], z_recv.at[k], near)
+
+    def from_far(k):
+        return remote(sendf.at[k], gotf.at[k], f_send.at[k], f_recv.at[k], far)
 
     def x_stage(i):
-        zt, j = steps[i]
         x_copies[i].wait_recv()
         total = own2[i, pl.ds(pl.multiple_of(x * quarter, quarter), quarter)] + got2[i].astype(jnp.float32)
-        if i % planes < planes - 1:
+        if i < own:
             sendz[i] = total.astype(jnp.bfloat16)
-            copy = remote(sendz.at[i], gotz.at[z, j], z_send.at[i], z_recv.at[z, j], at(zt, x, c))
-            copy.start()
-            sends.append(copy)
+            copy = from_near(i)
         else:
-            mine.append(total)
-
-    def finish(j):
-        total = mine[j]
-        for zz in others:
-            remote(sendz.at[0], gotz.at[zz, j], z_send.at[0], z_recv.at[zz, j], at(zz, x, c)).wait_recv()
-            total = total + gotz[zz, j].astype(jnp.float32)
-        gathered[z * per + j] = total.astype(jnp.bfloat16)
-        block = gathered.at[z * per + j]
-        for k in reversed(range(len(others))):
-            zz = others[k]
-            copy = remote(block, block, a_send.at[k, j], a_recv.at[z, j], at(zz, x, c))
-            copy.start()
-            sends.append(copy)
-
-    last = count - 1
+            k = i - own
+            from_near(k).wait_recv()
+            total = total + gotz[k].astype(jnp.float32)
+            own3[k] = total
+            sendf[k] = total.astype(jnp.bfloat16)
+            copy = from_far(k)
+        copy.start()
+        sends.append(copy)
+
+    def finish(k):
+        from_far(k).wait_recv()
+        block = gathered.at[mine + k]
+        gathered[mine + k] = (own3[k] + gotf[k].astype(jnp.float32)).astype(jnp.bfloat16)
+        copy = remote(block, block, a_send.at[k], a_recv.at[k], near)
+        copy.start()
+        sends.append(copy)
 
     def after(i):
         start_core(i)
@@ -177,7 +180,7 @@
             loads[i + AHEAD].start()
         partial_sum(i)
         if i == 0:
-            pl.semaphore_wait(barrier, len(mates) + len(others))
+            pl.semaphore_wait(barrier, len(mates) + 2)
             times_load.wait()
             for m, (xx, cc) in enumerate(mates):
                 copy = remote(times, times_all.at[q], t_send.at[m], t_recv.at[q], at(z, xx, cc))
@@ -188,15 +191,11 @@
         core_stage(i)
     for i in range(count - LAG_X, count):
         x_stage(i)
-        if i == count - LAG_X + 1:
-            for j in range(per - 1):
-                finish(j)
-    finish(per - 1)
-
-    for j in range(per):
-        for zz in others:
-            there = gathered.at[zz * per + j]
-            remote(there, there, a_send.at[0, j], a_recv.at[zz, j], at(zz, x, c)).wait_recv()
+    for k in range(own):
+        finish(k)
+    for k in range(own):
+        there = gathered.at[theirs + k]
+        remote(there, there, a_send.at[k], a_recv.at[k], near).wait_recv()
 
     for m, (xx, cc) in enumerate(mates):
         other = 2 * cc + xx
@@ -217,8 +216,7 @@
 
 def pair_elementals(eigvecs, momentum, times, devices):
     slices, _, colors, width, sites = eigvecs.shape
-    planes = devices // 4
-    per = slices // planes
+    own = slices // 2
     half, quarter, both = width // 2, width // 4, 2 * width
     bf, f32 = jnp.bfloat16, jnp.float32
     dma = pltpu.SemaphoreType.DMA
@@ -239,8 +237,11 @@
             pltpu.VMEM((slices, half, both), f32),
             pltpu.VMEM((slices, half, both), bf),
             pltpu.VMEM((slices, quarter, both), bf),
-            pltpu.VMEM((slices, quarter, both), bf),
-            pltpu.VMEM((planes, per, quarter, both), bf),
+            pltpu.VMEM((own, quarter, both), bf),
+            pltpu.VMEM((own, quarter, both), bf),
+            pltpu.VMEM((own, quarter, both), f32),
+            pltpu.VMEM((own, quarter, both), bf),
+            pltpu.VMEM((own, quarter, both), bf),
             pltpu.VMEM((slices, quarter, both), bf),
             pltpu.VMEM((3, 2, quarter, both), bf),
             pltpu.SMEM((4, 1, 2), jnp.int32),
@@ -249,8 +250,8 @@
             dma((2,)),
             dma((slices,)),
             dma((slices,)), dma((slices,)), dma((slices,)), dma((slices,)),
-            dma((slices,)), dma((planes, per)),
-            dma((planes, per)), dma((planes, per)),
+            dma((own,)), dma((own,)), dma((own,)), dma((own,)),
+            dma((own,)), dma((own,)),
             dma((3,)), dma((4,)),
             dma((3,)), dma((4,)),
         ],

time: 35.1 us -> 34 us (0.969)
  Pallas kernels: 35 us -> 33.8 us
    pallas_call x1, Pallas kernels: 30.4 us -> 29.2 us  [pair_elementals(): pl.pallas_call(functools.partial(elemental_kernel, devices), out_shape=ja...]
where the time goes in v2:
time: 34 us; the launch traced here: 33.8 us
  Pallas kernels  33.8 us (99%)
    pallas_call x1, Pallas kernels, pair_elementals(): pl.pallas_call(functools.partial(elemental_kernel, devices), out_shape=ja...  29.2 us
    pallas_call x1, Pallas kernels, meson_blocks(): pl.pallas_call(blocks_kernel, out_shape=jax.ShapeDtypeStruct(peram.shape,...  4.57 us

profile of v2, /device:TPU:1, one launch (start us, length us, event | category | flops | bytes accessed | tf_op | source)
XLA Modules:
  0.0 33.8 jit_solution(17169380773690287554)
XLA Ops:
  0.0 0.0 copy-start
  0.0 29.2 %shard_map.46.elementals = bf16[4,2,48,384]{3,2,1,0:T(8,128)(2,1)S(1)} custom-call(s32[3]{0:T(128)} %mom_hbm.1, s32[1,2]{1,0:T(1,128)} %times_hbm.1, bf16[8,2,3,192,512]{4,3,2,1,0:T(8,128)(2,1)} %eig.1), custom_call_target="tpu_custom_call" | custom-call | tf_op jit(solution)/shard_map/pallas_call | solution.py:223
  29.2 0.0 copy-done
  29.2 4.6 %shard_map.47 = bf16[1,2,768,768]{3,2,1,0:T(8,128)(2,1)} custom-call(bf16[4,2,48,384]{3,2,1,0:T(8,128)(2,1)S(1)} %shard_map.46.elementals, bf16[1,2,768,768]{3,2,1,0:T(8,128)(2,1)S(1)} %copy-done), custom_call_target="tpu_custom_call" | custom-call | tf_op jit(solution)/shard_map/pallas_call | solution.py:300
Async XLA Ops:
  0.0 29.2 %copy-start = (bf16[1,2,768,768]{3,2,1,0:T(8,128)(2,1)S(1)}, bf16[1,2,768,768]{3,2,1,0:T(8,128)(2,1)}, u32[]{:S(2)}) copy-start(bf16[1,2,768,768]{3,2,1,0:T(8,128)(2,1)} %peram.1) | copy-start | bytes 7077892
